TPU v7x, 32 devices: a whole 2x2x4 slice. The times are simulated.
32 devices in a mesh: row: 2 (over x), col: 4 (over y, core), layer: 4 (over z).
Axes of the slice: x: 2, y: 2, z: 4, core: 2. Of those that a mesh axis runs over, the one named last changes fastest.
Arguments:
- flow_matrix: float32 [2048, 2048], P('row', ('layer', 'col')), may hold values from 0.0009 to 310, as said below
- regularizer: float32 [2048, 2048], P(('layer', 'row'), 'col'), may hold values from 0.001 to 1
- pattern: int32 [8, 8], replicated, may hold values from 0 to 1, as said below
Outputs:
- inflated: float32 [2048, 2048], P(('row', 'layer'), 'col')
Inputs may be any that keep to these rules, and one draw needn't show every extreme that they name: `flow_matrix`: entries are positive. `pattern`: each entry is 0 or 1; every diagonal entry is 1.
All inputs are finite; a program needn't handle non-finite values.
Results may differ from a plain program's by a relative error of at most 0.000098.
Values sent between devices are 32-bit elements; how exact they have to be, the bound alone decides.
No kernel may reach another device: no remote copies, remote signals or barrier semaphores. Data moves between devices by JAX's collectives and lax.ppermute only.
A program may use at most 64 MiB of HBM per device.

v0:
```python
import jax
import jax.numpy as jnp
from jax import lax
from jax.sharding import PartitionSpec as P

TILE = 256


def keep_tiles(values, pattern, row_start, col_start):
    tile_count = pattern.shape[0]
    row_tile = (row_start + lax.iota(jnp.int32, values.shape[0])) // TILE
    col_tile = (col_start + lax.iota(jnp.int32, values.shape[1])) // TILE
    tile_ids = lax.iota(jnp.int32, tile_count)
    row_pick = (row_tile[:, None] == tile_ids[None, :]).astype(jnp.float32)
    col_pick = (col_tile[:, None] == tile_ids[None, :]).astype(jnp.float32)
    pattern_rows = jnp.dot(
        row_pick,
        pattern.astype(jnp.float32),
        precision=lax.Precision.HIGHEST,
        preferred_element_type=jnp.float32,
    )
    chosen = jnp.dot(
        pattern_rows,
        col_pick.T,
        precision=lax.Precision.HIGHEST,
        preferred_element_type=jnp.float32,
    )
    return values * chosen


def shards(flow_matrix, regularizer, pattern):
    order_total = flow_matrix.shape[0] * lax.axis_size("row")
    left_whole = lax.all_gather(flow_matrix, "col", axis=1, tiled=True)
    partial_value = jnp.dot(
        left_whole,
        lax.all_gather(regularizer, "row", axis=0, tiled=True),
        precision=lax.Precision.HIGHEST,
        preferred_element_type=jnp.float32,
    )
    own_count = partial_value.shape[0] // lax.axis_size("layer")
    col_start = lax.axis_index("col") * partial_value.shape[1]
    expanded = lax.psum_scatter(partial_value, "layer", scatter_dimension=0, tiled=True)
    row_start = lax.axis_index("row") * partial_value.shape[0] + lax.axis_index("layer") * own_count
    pruned = keep_tiles(expanded, pattern, row_start, col_start)
    squared = pruned * pruned
    totals = lax.psum(jnp.sum(squared, axis=0), ("row", "layer"))
    inflated = squared / totals[None, :] * order_total
    return inflated


def solution(mesh):
    return jax.shard_map(
        shards,
        mesh=mesh,
        in_specs=(P("row", ("layer", "col")), P(("layer", "row"), "col"), P()),
        out_specs=P(("row", "layer"), "col"),
        check_vma=False,
    )
```

profile of v0, /device:TPU:0, one launch (start us, length us, event | category | flops | bytes accessed | tf_op | source)
XLA Modules:
  0.0 136.4 jit_solution(12964221598717887879)
XLA Ops:
  6.5 0.0 all-gather.5.cloned.1.call-start
  6.5 0.7 all-gather.5.cloned.1.call-update
  7.3 0.0 all-gather.3.cloned.1.call-start
  7.3 0.7 all-gather.3.cloned.1.call-update
  8.0 0.0 reduce-scatter.2.cloned.1.call-start
  8.1 24.9 %all-gather.5.cloned.1.call-done = f32[512,512]{1,0:T(8,128)} async-done(((f32[256,512]{1,0:T(8,128)}), f32[512,512]{1,0:T(8,128)}) %all-gather.5.cloned.1.call-update) | async-done | bytes 1048592 | tf_op jit(solution)/shard_map/all_gather | solution.py:36
  32.9 24.4 %all-gather.3.cloned.1.call-done = f32[1024,512]{1,0:T(8,128)} async-done(((f32[1024,128]{1,0:T(8,128)}), f32[1024,512]{1,0:T(8,128)}) %all-gather.3.cloned.1.call-update) | async-done | bytes 2097168 | tf_op jit(solution)/shard_map/all_gather | solution.py:33
  57.3 6.6 %fusion.9 = f32[1024,512]{1,0:T(8,128)} fusion(f32[1024,512]{1,0:T(8,128)} %all-gather.3.cloned.1.call-done, f32[512,512]{1,0:T(8,128)} %all-gather.5.cloned.1.call-done), kind=kOutput, calls=%fused_computation.23 | convolution fusion | flops 3221225472 | bytes 5242880 | tf_op jit(solution)/shard_map/dot_general | solution.py:34
  63.9 0.0 copy-start
  63.9 0.0 reduce-scatter.2.cloned.1.call-update
  64.0 0.6 copy-done
  64.6 0.3 fusion.2
  64.9 42.9 %reduce-scatter.2.cloned.1.call-done = f32[256,512]{1,0:T(8,128)} async-done(((f32[1024,512]{1,0:T(8,128)}), f32[256,512]{1,0:T(8,128)}) %reduce-scatter.2.cloned.1.call-update) | async-done | bytes 524304 | tf_op jit(solution)/shard_map/reduce_scatter | solution.py:42
  107.8 1.6 %fusion.8 = (f32[512]{0:T(512)S(1)}, f32[256,512]{1,0:T(8,128)S(1)}) fusion(f32[256,512]{1,0:T(8,128)} %reduce-scatter.2.cloned.1.call-done, f32[256,8]{1,0:T(8,128)S(1)} %fusion.2, s32[512]{0:T(512)S(1)} %add_select_fusion), kind=kOutput, calls=%fused_computation.22 | convolution fusion | flops 12979712 | bytes 1060864 | tf_op jit(solution)/shard_map/dot_general | solution.py:22
  109.3 19.7 %psum.7 = f32[512]{0:T(512)S(1)} all-reduce(f32[512]{0:T(512)S(1)} %get-tuple-element.5), channel_id=1, replica_groups=mesh['row'=2,'col'=4,'layer'=4] {'row','layer'}, use_global_device_ids=true, to_apply=%region_2.3 | all-reduce | flops 512 | bytes 4096 | tf_op jit(solution)/shard_map/psum | solution.py:46
  129.0 0.9 divide_multiply_fusion
  (2 shorter events, 0.0 us)
Async XLA Ops:
  6.5 26.4 %all-gather.5.cloned.1.call-start = ((), (), s32[]{:S(2)}) async-start(), calls=%async_computation.2 | async-start | bytes 1572864 | tf_op jit(solution)/shard_map/all_gather | solution.py:36
  7.3 50.1 %all-gather.3.cloned.1.call-start = ((), (), s32[]{:S(2)}) async-start(), calls=%async_computation.1 | async-start | bytes 2621440 | tf_op jit(solution)/shard_map/all_gather | solution.py:33
  8.0 99.8 %reduce-scatter.2.cloned.1.call-start = ((), (), s32[]{:S(2)}) async-start(), calls=%async_computation.3 | async-start | bytes 2621440 | tf_op jit(solution)/shard_map/reduce_scatter | solution.py:42
  63.9 0.7 copy-start
Sparse Core Ops, SparseCore 0:
  8.9 23.9 all-gather.4
  34.5 22.8 all-gather.2
  64.1 43.6 reduce-scatter.1
where the time goes:
time: 137 us; the launch traced here: 136 us
  waiting for transfers between devices  93.5 us (68%)
  blocking collectives  19.7 us (14%)
  between operations  13.1 us (10%)
  matrix products  8.44 us (6%)
    reduce_scatter x1, waiting for transfers between devices, shards(): lax.psum_scatter(partial_value, 'layer', scatter_dimension=0, tiled=True)  42.9 us
    all_gather x1, waiting for transfers between devices, shards(): lax.all_gather(regularizer, 'row', axis=0, tiled=True)  24.9 us
    all_gather x1, waiting for transfers between devices, shards(): left_whole = lax.all_gather(flow_matrix, 'col', axis=1, tiled=True)  24.4 us
    psum x1, blocking collectives, shards(): totals = lax.psum(jnp.sum(squared, axis=0), ('row', 'layer'))  19.7 us
    dot_general x1, matrix products, shards(): jnp.dot(left_whole, lax.all_gather(regularizer, 'row', axis=0, tiled=True...  6.63 us
  transfers between devices with their start and end apart: 3, of which 3 were waited for; matrix products, arithmetic and copies ran while one was open for 0% of the time, Pallas kernels for 0%

commit v1 on v0

--- a/solution.py
+++ b/solution.py
@@ -1,9 +1,17 @@
+import functools
 import jax
 import jax.numpy as jnp
 from jax import lax
 from jax.sharding import PartitionSpec as P
 
 TILE = 256
+
+
+def part_the_modes(frame_in, mesh_dim):
+    return jnp.sum(lax.all_gather(frame_in, mesh_dim), 0)
+
+
+return_all_roads = functools.partial(part_the_modes, mesh_dim=("row", "layer"))
 
 
 def keep_tiles(values, pattern, row_start, col_start):
@@ -43,7 +51,7 @@
     row_start = lax.axis_index("row") * partial_value.shape[0] + lax.axis_index("layer") * own_count
     pruned = keep_tiles(expanded, pattern, row_start, col_start)
     squared = pruned * pruned
-    totals = lax.psum(jnp.sum(squared, axis=0), ("row", "layer"))
+    totals = return_all_roads(jnp.sum(squared, axis=0))
     inflated = squared / totals[None, :] * order_total
     return inflated
 

time: 137 us -> 144 us (1.051)
  blocking collectives: 19.7 us -> 27 us
    all_gather x0 -> x1, blocking collectives: none -> 27 us  [part_the_modes(): return jnp.sum(lax.all_gather(frame_in, mesh_dim), 0)]
    psum x1 -> x0, blocking collectives: 19.7 us -> none  [shards(): totals = lax.psum(jnp.sum(squared, axis=0), ('row', 'layer'))]
where the time goes in v1:
time: 144 us
  waiting for transfers between devices  93.5 us (65%)
  blocking collectives  27 us (19%)
  between operations  13.1 us (9%)
  matrix products  8.44 us (6%)
    reduce_scatter x1, waiting for transfers between devices, shards(): lax.psum_scatter(partial_value, 'layer', scatter_dimension=0, tiled=True)  42.9 us
    all_gather x1, blocking collectives, part_the_modes(): return jnp.sum(lax.all_gather(frame_in, mesh_dim), 0)  27 us
    all_gather x1, waiting for transfers between devices, shards(): lax.all_gather(regularizer, 'row', axis=0, tiled=True)  24.9 us
    all_gather x1, waiting for transfers between devices, shards(): left_whole = lax.all_gather(flow_matrix, 'col', axis=1, tiled=True)  24.4 us
    dot_general x1, matrix products, shards(): jnp.dot(left_whole, lax.all_gather(regularizer, 'row', axis=0, tiled=True...  6.63 us
  transfers between devices with their start and end apart: 3, of which 3 were waited for; matrix products, arithmetic and copies ran while one was open for 0% of the time, Pallas kernels for 0%

profile of v1, /device:TPU:0, one launch (start us, length us, event | category | flops | bytes accessed | tf_op | source)
XLA Modules:
  0.0 143.8 jit_solution(2477804963000191579)
XLA Ops:
  6.5 0.0 all-gather.7.cloned.1.call-start
  6.5 0.7 all-gather.7.cloned.1.call-update
  7.3 0.0 all-gather.5.cloned.1.call-start
  7.3 0.7 all-gather.5.cloned.1.call-update
  8.0 0.0 reduce-scatter.2.cloned.1.call-start
  8.1 24.9 %all-gather.7.cloned.1.call-done = f32[512,512]{1,0:T(8,128)} async-done(((f32[256,512]{1,0:T(8,128)}), f32[512,512]{1,0:T(8,128)}) %all-gather.7.cloned.1.call-update) | async-done | bytes 1048592 | tf_op jit(solution)/shard_map/all_gather | solution.py:44
  32.9 24.4 %all-gather.5.cloned.1.call-done = f32[1024,512]{1,0:T(8,128)} async-done(((f32[1024,128]{1,0:T(8,128)}), f32[1024,512]{1,0:T(8,128)}) %all-gather.5.cloned.1.call-update) | async-done | bytes 2097168 | tf_op jit(solution)/shard_map/all_gather | solution.py:41
  57.3 6.6 %fusion.9 = f32[1024,512]{1,0:T(8,128)} fusion(f32[1024,512]{1,0:T(8,128)} %all-gather.5.cloned.1.call-done, f32[512,512]{1,0:T(8,128)} %all-gather.7.cloned.1.call-done), kind=kOutput, calls=%fused_computation.23 | convolution fusion | flops 3221225472 | bytes 5242880 | tf_op jit(solution)/shard_map/dot_general | solution.py:42
  63.9 0.0 copy-start
  63.9 0.0 reduce-scatter.2.cloned.1.call-update
  64.0 0.6 copy-done
  64.6 0.3 fusion.2
  64.9 42.9 %reduce-scatter.2.cloned.1.call-done = f32[256,512]{1,0:T(8,128)} async-done(((f32[1024,512]{1,0:T(8,128)}), f32[256,512]{1,0:T(8,128)}) %reduce-scatter.2.cloned.1.call-update) | async-done | bytes 524304 | tf_op jit(solution)/shard_map/reduce_scatter | solution.py:50
  107.8 1.6 %fusion.8 = (f32[512]{0:T(512)S(1)}, f32[256,512]{1,0:T(8,128)S(1)}) fusion(f32[256,512]{1,0:T(8,128)} %reduce-scatter.2.cloned.1.call-done, f32[256,8]{1,0:T(8,128)S(1)} %fusion.2, s32[512]{0:T(512)S(1)} %add_select_fusion), kind=kOutput, calls=%fused_computation.22 | convolution fusion | flops 12979712 | bytes 1060864 | tf_op jit(solution)/shard_map/dot_general | solution.py:30
  109.3 27.0 %all-gather.1 = f32[8,1,512]{2,1,0:T(1,128)S(1)} all-gather(f32[1,1,512]{2,1,0:T(1,128)S(1)} %bitcast.4), channel_id=2, replica_groups=mesh['row'=2,'col'=4,'layer'=4] {'row','layer'}, dimensions={0}, use_global_device_ids=true | all-gather | bytes 18432 | tf_op jit(solution)/shard_map/all_gather | solution.py:11
  136.4 0.9 divide_multiply_fusion
  (3 shorter events, 0.0 us)
Async XLA Ops:
  6.5 26.4 %all-gather.7.cloned.1.call-start = ((), (), s32[]{:S(2)}) async-start(), calls=%async_computation.2 | async-start | bytes 1572864 | tf_op jit(solution)/shard_map/all_gather | solution.py:44
  7.3 50.1 %all-gather.5.cloned.1.call-start = ((), (), s32[]{:S(2)}) async-start(), calls=%async_computation.1 | async-start | bytes 2621440 | tf_op jit(solution)/shard_map/all_gather | solution.py:41
  8.0 99.8 %reduce-scatter.2.cloned.1.call-start = ((), (), s32[]{:S(2)}) async-start(), calls=%async_computation.3 | async-start | bytes 2621440 | tf_op jit(solution)/shard_map/reduce_scatter | solution.py:50
  63.9 0.7 copy-start
Sparse Core Ops, SparseCore 0:
  8.9 23.9 all-gather.6
  34.5 22.8 all-gather.4
  64.1 43.6 reduce-scatter.1

commit v2 on v0

--- a/solution.py
+++ b/solution.py
@@ -4,6 +4,17 @@
 from jax.sharding import PartitionSpec as P
 
 TILE = 256
+
+
+def around_the_ring(value, name, dim):
+    peers = lax.axis_size(name)
+    route = [(i, (i + 1) % peers) for i in range(peers)]
+    blocks = [value]
+    for far in range(1, peers):
+        blocks = [lax.ppermute(blocks[0], name, route), *blocks]
+    whole = jnp.concatenate(blocks, axis=dim)
+    shift = (lax.axis_index(name) + 1) * blocks[-1].shape[dim]
+    return jnp.roll(whole, shift, axis=dim)
 
 
 def keep_tiles(values, pattern, row_start, col_start):
@@ -30,7 +41,7 @@
 
 def shards(flow_matrix, regularizer, pattern):
     order_total = flow_matrix.shape[0] * lax.axis_size("row")
-    left_whole = lax.all_gather(flow_matrix, "col", axis=1, tiled=True)
+    left_whole = around_the_ring(flow_matrix, "col", 1)
     partial_value = jnp.dot(
         left_whole,
         lax.all_gather(regularizer, "row", axis=0, tiled=True),

time: 137 us -> 129 us (0.942)
  waiting for transfers between devices: 93.5 us -> 76.8 us
  local copies, waits for them, and re-layouts: 0.62 us -> 8.06 us
    ppermute x0 -> x3, waiting for transfers between devices: none -> 26.2 us  [around_the_ring(): blocks = [lax.ppermute(blocks[0], name, route), *blocks]]
    all_gather x1 -> x0, waiting for transfers between devices: 24.4 us -> none  [shards(): left_whole = lax.all_gather(flow_matrix, 'col', axis=1, tiled=True)]
    all_gather x1, waiting for transfers between devices: 24.9 us -> 7.08 us  [shards(): lax.all_gather(regularizer, 'row', axis=0, tiled=True)]
    unnamed x2 -> x11, local copies, waits for them, and re-layouts: 0.62 us -> 7.19 us
    unnamed x3 -> x2, waiting for transfers between devices: 1.42 us -> 0.03 us
  transfers between devices with their start and end apart: 3 -> 5, of which waited for: 3 -> 5; matrix products, arithmetic and copies ran while one was open for 0% -> 6% of each run, Pallas kernels for 0% -> 0%
where the time goes in v2:
time: 129 us
  waiting for transfers between devices  76.8 us (60%)
  blocking collectives  19.7 us (15%)
  between operations  13.5 us (10%)
  matrix products  8.41 us (7%)
  local copies, waits for them, and re-layouts  8.06 us (6%)
  other arithmetic  1.97 us (2%)
    reduce_scatter x1, waiting for transfers between devices, shards(): lax.psum_scatter(partial_value, 'layer', scatter_dimension=0, tiled=True)  43.5 us
    ppermute x3, waiting for transfers between devices, around_the_ring(): blocks = [lax.ppermute(blocks[0], name, route), *blocks]  26.2 us
    psum x1, blocking collectives, shards(): totals = lax.psum(jnp.sum(squared, axis=0), ('row', 'layer'))  19.7 us
    unnamed x11, local copies, waits for them, and re-layouts  7.19 us
    all_gather x1, waiting for transfers between devices, shards(): lax.all_gather(regularizer, 'row', axis=0, tiled=True)  7.08 us
    dot_general x1, matrix products, shards(): jnp.dot(left_whole, lax.all_gather(regularizer, 'row', axis=0, tiled=True...  6.6 us
  transfers between devices with their start and end apart: 5, of which 5 were waited for; matrix products, arithmetic and copies ran while one was open for 6% of the time, Pallas kernels for 0%

profile of v2, /device:TPU:0, one launch (start us, length us, event | category | flops | bytes accessed | tf_op | source)
XLA Modules:
  0.0 128.9 jit_solution(17380092334435893907)
XLA Ops:
  6.5 0.0 copy-start
  6.5 0.0 all-gather.2.cloned.1.call-start
  6.5 0.5 collective-permute-start
  7.0 9.1 %collective-permute-done = f32[1024,128]{1,0:T(8,128)S(1)} collective-permute-done((f32[1024,128]{1,0:T(8,128)}, f32[1024,128]{1,0:T(8,128)S(1)}, u32[]{:S(2)}, u32[]{:S(2)}) %collective-permute-start) | collective-permute-done | bytes 524320 | tf_op jit(solution)/shard_map/ppermute | solution.py:14
  16.1 0.0 collective-permute-start.1
  16.1 8.6 %collective-permute-done.1 = f32[1024,128]{1,0:T(8,128)S(1)} collective-permute-done((f32[1024,128]{1,0:T(8,128)S(1)}, f32[1024,128]{1,0:T(8,128)S(1)}, u32[]{:S(2)}, u32[]{:S(2)}) %collective-permute-start.1) | collective-permute-done | bytes 524320 | tf_op jit(solution)/shard_map/ppermute | solution.py:14
  24.7 0.0 collective-permute-start.2
  24.7 0.0 all-gather.2.cloned.1.call-update
  24.8 0.0 reduce-scatter.2.cloned.1.call-start
  24.8 8.5 %collective-permute-done.2 = f32[1024,128]{1,0:T(8,128)S(1)} collective-permute-done((f32[1024,128]{1,0:T(8,128)S(1)}, f32[1024,128]{1,0:T(8,128)S(1)}, u32[]{:S(2)}, u32[]{:S(2)}) %collective-permute-start.2) | collective-permute-done | bytes 524320 | tf_op jit(solution)/shard_map/ppermute | solution.py:14
  33.3 0.9 constant_dynamic-update-slice_fusion.7
  34.3 0.9 constant_dynamic-update-slice_fusion.6
  35.1 0.9 constant_dynamic-update-slice_fusion.5
  36.0 1.9 %constant_dynamic-update-slice_fusion.4 = f32[1024,1024]{1,0:T(8,128)} fusion(f32[1024,1024]{1,0:T(8,128)} %constant_dynamic-update-slice_fusion.5, f32[1024,128]{1,0:T(8,128)} %param.3), kind=kLoop, calls=%fused_computation.15 | loop fusion | bytes 1048576
  37.9 0.9 constant_dynamic-update-slice_fusion.3
  38.8 0.9 constant_dynamic-update-slice_fusion.2
  39.6 0.9 constant_dynamic-update-slice_fusion.1
  40.5 0.0 copy-done
  40.5 0.0 copy-start.1
  40.5 0.9 constant_dynamic-update-slice_fusion
  41.4 7.1 %all-gather.2.cloned.1.call-done = f32[512,512]{1,0:T(8,128)} async-done(((f32[256,512]{1,0:T(8,128)}), f32[512,512]{1,0:T(8,128)}) %all-gather.2.cloned.1.call-update) | async-done | bytes 1048592 | tf_op jit(solution)/shard_map/all_gather | solution.py:47
  48.5 6.6 %fusion = f32[1024,512]{1,0:T(8,128)} fusion(f32[512,512]{1,0:T(8,128)} %all-gather.2.cloned.1.call-done, f32[1024,1024]{1,0:T(8,128)} %constant_dynamic-update-slice_fusion, s32[]{:T(128)S(6)} %select_n.32), kind=kOutput, calls=%fused_computation | convolution fusion | flops 3221225472 | bytes 5242884 | tf_op jit(solution)/shard_map/dot_general | solution.py:45
  55.1 0.0 reduce-scatter.2.cloned.1.call-update
  55.1 0.0 copy-done.1
  55.2 0.3 fusion.5
  55.4 43.5 %reduce-scatter.2.cloned.1.call-done = f32[256,512]{1,0:T(8,128)} async-done(((f32[1024,512]{1,0:T(8,128)}), f32[256,512]{1,0:T(8,128)}) %reduce-scatter.2.cloned.1.call-update) | async-done | bytes 524304 | tf_op jit(solution)/shard_map/reduce_scatter | solution.py:53
  98.9 1.6 %fusion.3 = (f32[512]{0:T(512)S(1)}, f32[256,512]{1,0:T(8,128)S(1)}) fusion(f32[256,512]{1,0:T(8,128)} %reduce-scatter.2.cloned.1.call-done, f32[256,8]{1,0:T(8,128)S(1)} %fusion.5, s32[512]{0:T(512)S(1)} %add_select_fusion), kind=kOutput, calls=%fused_computation.6 | convolution fusion | flops 12979712 | bytes 1060864 | tf_op jit(solution)/shard_map/dot_general | solution.py:33
  100.4 19.7 %psum.7 = f32[512]{0:T(512)S(1)} all-reduce(f32[512]{0:T(512)S(1)} %get-tuple-element.5), channel_id=1, replica_groups=mesh['row'=2,'col'=4,'layer'=4] {'row','layer'}, use_global_device_ids=true, to_apply=%region_2.3 | all-reduce | flops 512 | bytes 4096 | tf_op jit(solution)/shard_map/psum | solution.py:57
  120.1 1.9 %divide_multiply_fusion = f32[256,512]{1,0:T(8,128)} fusion(f32[512]{0:T(512)S(1)} %psum.7, f32[256,512]{1,0:T(8,128)} %reduce-scatter.2.cloned.1.call-done, f32[256,512]{1,0:T(8,128)S(1)} %get-tuple-element.6), kind=kLoop, calls=%fused_computation.2 | loop fusion | flops 524288 | bytes 1574912 | tf_op jit(solution)/shard_map/mul | solution.py:58
  (2 shorter events, 0.0 us)
Async XLA Ops:
  6.5 34.0 %copy-start = (f32[1024,128]{1,0:T(8,128)S(1)}, f32[1024,128]{1,0:T(8,128)}, u32[]{:S(2)}) copy-start(f32[1024,128]{1,0:T(8,128)} %param.3) | copy-start | bytes 1572868
  6.5 41.9 %all-gather.2.cloned.1.call-start = ((), (), s32[]{:S(2)}) async-start(), calls=%async_computation.1 | async-start | bytes 1572864 | tf_op jit(solution)/shard_map/all_gather | solution.py:47
  6.5 9.6 %collective-permute-start = (f32[1024,128]{1,0:T(8,128)}, f32[1024,128]{1,0:T(8,128)S(1)}, u32[]{:S(2)}, u32[]{:S(2)}) collective-permute-start(f32[1024,128]{1,0:T(8,128)} %param.3), channel_id=1, source_target_pairs={{0,4},{4,8},{8,12},{12,0},{1,5},{5,9},{9,13},{13,1},{2,6},{6,10},{... | collective-permute-start | bytes 1572872 | tf_op jit(solution)/shard_map/ppermute | solution.py:14
  16.1 8.6 %collective-permute-start.1 = (f32[1024,128]{1,0:T(8,128)S(1)}, f32[1024,128]{1,0:T(8,128)S(1)}, u32[]{:S(2)}, u32[]{:S(2)}) collective-permute-start(f32[1024,128]{1,0:T(8,128)S(1)} %collective-permute-done), channel_id=1, source_target_pairs={{0,4},{4,8},{8,12},{12,0},{1,5},{5,9},{9,13},{13,1},{2,6},{6,10},{... | collective-permute-start | bytes 1572872 | tf_op jit(solution)/shard_map/ppermute | solution.py:14
  24.7 8.6 %collective-permute-start.2 = (f32[1024,128]{1,0:T(8,128)S(1)}, f32[1024,128]{1,0:T(8,128)S(1)}, u32[]{:S(2)}, u32[]{:S(2)}) collective-permute-start(f32[1024,128]{1,0:T(8,128)S(1)} %collective-permute-done.1), channel_id=1, source_target_pairs={{0,4},{4,8},{8,12},{12,0},{1,5},{5,9},{9,13},{13,1},{2,6},{6,10},{... | collective-permute-start | bytes 1572872 | tf_op jit(solution)/shard_map/ppermute | solution.py:14
  24.8 74.1 %reduce-scatter.2.cloned.1.call-start = ((), (), s32[]{:S(2)}) async-start(), calls=%async_computation.2 | async-start | bytes 2621440 | tf_op jit(solution)/shard_map/reduce_scatter | solution.py:53
  40.5 14.6 %copy-start.1 = (s32[8,8]{1,0:T(8,128)S(1)}, s32[8,8]{1,0:T(8,128)}, u32[]{:S(2)}) copy-start(s32[8,8]{1,0:T(8,128)} %param.5) | copy-start | bytes 772
Sparse Core Ops, SparseCore 0:
  24.9 23.5 all-gather.1
  55.2 43.6 reduce-scatter.1
